TPU v7x, 128 devices: a whole 4x4x4 slice. The times are simulated.
128 devices in a mesh: section: 2 (over core), dp: 16 (over y, x), mp: 4 (over z).
Axes of the slice: x: 4, y: 4, z: 4, core: 2. Of those that a mesh axis runs over, the one named last changes fastest.
Arguments:
- patches: bfloat16 [8192, 1280], P(('section', 'dp', 'mp')), may hold values from -6 to 6
- image_units: int32 [128, 3], P(('section', 'dp', 'mp')), may hold values from 1 to 8, 16 in all within a row
- v_gain: float32 [1280], replicated, may hold values from 0.5 to 1.5
- v_qkv: bfloat16 [1280, 3840], replicated, may hold values from -0.15625 to 0.15625
- v_out: bfloat16 [1280, 1280], replicated, may hold values from -0.15625 to 0.15625
- merge_gain: float32 [1280], replicated, may hold values from 0.5 to 1.5
- w_merge: bfloat16 [5120, 8192], P('dp', 'mp'), may hold values from -0.078125 to 0.078125
- routes: int32 [2048, 1], P(('section', 'dp', 'mp')), may hold values from 0 to 15; in each aligned block of 1024 rows (0 to 1023, 1024 to 2047, ...) at most 128 rows name the same one
- text: bfloat16 [4096, 8192], P(('section', 'dp'), 'mp'), may hold values from -6 to 6
- seq_lengths: int32 [32, 3], P(('section', 'dp')), may hold values from 1 to 64, 128 in all within a row
- lang_gain: float32 [2, 8192], P('section'), may hold values from 0.5 to 1.5
- w_qkv: bfloat16 [2, 8192, 5120], P('section', 'dp', 'mp'), may hold values from -0.0625 to 0.0625
- wo_t: bfloat16 [2, 8192, 4096], P('section', 'dp', 'mp'), may hold values from -0.09375 to 0.09375
- row_grads: bfloat16 [4096, 8192], P(('section', 'dp'), 'mp'), may hold values from -6 to 6
Outputs:
- final_hidden: bfloat16 [4096, 8192], P(('section', 'dp'), 'mp')
- merged_grads: bfloat16 [2048, 8192], P(('section', 'dp', 'mp'))
Inputs may be any that keep to these rules, and one draw needn't show every extreme that they name: `image_units`: each row sums to 16. `routes`: among the 1024 rows of one section index (aligned blocks), at most 128 name one group; in some section index one group is named by exactly 128. `seq_lengths`: each row sums to 128.
All inputs are finite; a program needn't handle non-finite values.
Results may differ from a plain program's by a relative error of at most 0.03.
Values may be sent and summed in bfloat16 or wider, within the bound.
A program may use at most 192 MiB of HBM per device.

v0:
```python
import math
import jax
import jax.numpy as jnp
from jax import lax
from jax.sharding import PartitionSpec as P

QH = 32
KVH = 4
HD = 128
VD = 1280
VH = 16
VHD = 80
MERGE = 4
EPSILON = 1e-06


def passed_along(value, axis, steps):
    count = lax.axis_size(axis)
    initial, last = (max(0, -steps), min(count, count - steps))
    return lax.ppermute(value, axis, [(source, source + steps) for source in range(initial, last)])


def broadcast(block, axis, owner):
    block = jnp.where(lax.axis_index(axis) == owner, block, jnp.zeros_like(block))
    return lax.psum(block, axis)


def layer_norm(values, norm_gain):
    values = values.astype(jnp.float32)
    centre = jnp.mean(values, axis=-1, keepdims=True)
    centred = values - centre
    variance = jnp.mean(centred * centred, axis=-1, keepdims=True)
    return centred * lax.rsqrt(variance + EPSILON) * norm_gain


def rms_norm(values, norm_gain):
    values = values.astype(jnp.float32)
    return (
        values * lax.rsqrt(jnp.mean(values * values, axis=-1, keepdims=True) + EPSILON) * norm_gain
    )


def segment_of(lengths, amount):
    boundary = jnp.cumsum(lengths.astype(jnp.int32))
    positions = jnp.arange(amount, dtype=jnp.int32)
    return jnp.sum((positions[:, None] >= boundary[None, :]).astype(jnp.int32), axis=1)


def vision_rows(patches, units, v_gain, v_qkv, v_out, merge_gain):
    amount = patches.shape[0]
    merged_count = amount // MERGE
    unit_image = segment_of(units, merged_count)
    image_ids = jnp.broadcast_to(unit_image[:, None], (merged_count, MERGE)).reshape(amount)
    v_normed = layer_norm(patches, v_gain).astype(jnp.bfloat16)
    projected = jnp.dot(v_normed, v_qkv, preferred_element_type=jnp.float32).astype(jnp.bfloat16)
    projected = projected.reshape(amount, 3, VH, VHD)
    scores = jnp.einsum(
        "qhd,khd->hqk", projected[:, 0], projected[:, 1], preferred_element_type=jnp.float32
    ) / math.sqrt(VHD)
    allowed = image_ids[:, None] == image_ids[None, :]
    scores = jnp.where(allowed[None], scores, -1e30)
    weights = jax.nn.softmax(scores, axis=-1).astype(jnp.bfloat16)
    attended = (
        jnp.einsum("hqk,khd->qhd", weights, projected[:, 2], preferred_element_type=jnp.float32)
        .astype(jnp.bfloat16)
        .reshape(amount, VD)
    )
    update = jnp.dot(attended, v_out, preferred_element_type=jnp.float32)
    v_hidden = (patches.astype(jnp.float32) + update).astype(jnp.bfloat16)
    merged = layer_norm(v_hidden, merge_gain).astype(jnp.bfloat16)
    return merged.reshape(merged_count, MERGE * VD)


def attend(projected, lengths):
    seq_rows = projected.shape[0]
    group_size = QH // KVH
    kv_here = projected.shape[1] // ((group_size + 2) * HD)
    heads_view = projected.reshape(seq_rows, kv_here, group_size + 2, HD)
    scores = jnp.einsum(
        "tkgd,skd->kgts",
        heads_view[:, :, :group_size],
        heads_view[:, :, group_size],
        preferred_element_type=jnp.float32,
    ) * (1.0 / math.sqrt(HD))
    seq_ids = segment_of(lengths, seq_rows)
    positions = jnp.arange(seq_rows, dtype=jnp.int32)
    allowed = (seq_ids[:, None] == seq_ids[None, :]) & (positions[:, None] >= positions[None, :])
    scores = jnp.where(allowed[None, None], scores, -1e30)
    weights = jax.nn.softmax(scores, axis=-1).astype(jnp.bfloat16)
    attended = jnp.einsum(
        "kgts,skd->tkgd",
        weights,
        heads_view[:, :, group_size + 1],
        preferred_element_type=jnp.float32,
    ).astype(jnp.bfloat16)
    return attended.reshape(seq_rows, kv_here * group_size * HD)


def shards(
    patches,
    image_units,
    v_gain,
    v_qkv,
    v_out,
    merge_gain,
    w_merge,
    routes,
    text,
    seq_lengths,
    lang_gain,
    w_qkv,
    wo_t,
    row_grads,
):
    merged = vision_rows(patches, image_units[0], v_gain, v_qkv, v_out, merge_gain)
    all_rows, all_routes = (
        lax.all_gather(merged, ("dp", "mp"), axis=0, tiled=True),
        lax.all_gather(routes, ("dp", "mp"), axis=0, tiled=True),
    )
    target = all_routes[:, 0]
    section_rows = target.shape[0]
    row_order = jnp.arange(section_rows, dtype=jnp.int32)
    matching = target[:, None] == target[None, :]
    position = jnp.sum(
        (matching & (row_order[:, None] > row_order[None, :])).astype(jnp.int32), axis=1
    )
    seq_rows = text.shape[0]
    slot_index = target * seq_rows + position
    group_here = lax.axis_index("dp")
    dp_count = lax.axis_size("dp")
    slice_width = w_merge.shape[0]
    row_slice = lax.dynamic_slice_in_dim(all_rows, group_here * slice_width, slice_width, 1)
    wanted = jnp.arange(seq_rows * lax.axis_size("dp"), dtype=jnp.int32)
    picker = (slot_index[None, :] == wanted[:, None]).astype(jnp.bfloat16)
    picked = jnp.dot(picker, row_slice, preferred_element_type=jnp.float32).astype(jnp.bfloat16)
    image_rows = lax.psum_scatter(
        jnp.dot(picked, w_merge, preferred_element_type=jnp.float32).astype(jnp.bfloat16),
        "dp",
        scatter_dimension=0,
        tiled=True,
    )
    present = jnp.sum((target == group_here).astype(jnp.int32))
    positions = jnp.arange(seq_rows, dtype=jnp.int32)
    entry_rows = jnp.where((positions < present)[:, None], image_rows, text)
    gathered = (
        lax.all_gather(w_qkv, "dp", axis=1, tiled=True),
        lax.all_gather(wo_t, "dp", axis=1, tiled=True),
    )
    qkv_weight = gathered[0][0]
    out_weight = gathered[1][0]
    norm_gain = lang_gain[0]
    sections = lax.axis_size("section")
    section_here = lax.axis_index("section")
    is_first = section_here == 0
    lengths_here = seq_lengths[0]
    entry_all, lengths_all = (
        lax.all_gather(entry_rows, "section", axis=0, tiled=True),
        lax.all_gather(seq_lengths, "section", axis=0, tiled=True),
    )
    carried = jnp.zeros_like(entry_rows)
    carried_lengths = lengths_here
    finished = []
    for section_step in range(2 * sections - 1):
        if section_step > 0:
            carried, carried_lengths = passed_along((carried, carried_lengths), "section", 1)
        if section_step < sections:
            incoming = entry_all[section_step * seq_rows : (section_step + 1) * seq_rows]
            incoming_lengths = lengths_all[section_step]
            carried = jnp.where(is_first, incoming, carried)
            carried_lengths = jnp.where(is_first, incoming_lengths, carried_lengths)
        features = lax.all_gather(carried, "mp", axis=1, tiled=True)
        normed = rms_norm(features, norm_gain).astype(jnp.bfloat16)
        projected = jnp.dot(normed, qkv_weight, preferred_element_type=jnp.float32)
        attended = attend(projected.astype(jnp.bfloat16), carried_lengths)
        partial_value = lax.dot_general(
            attended, out_weight, (((1,), (1,)), ((), ())), preferred_element_type=jnp.float32
        )
        update = lax.psum_scatter(
            partial_value.astype(jnp.bfloat16), "mp", scatter_dimension=1, tiled=True
        ).astype(jnp.float32)
        carried = (carried.astype(jnp.float32) + update).astype(jnp.bfloat16)
        if section_step >= sections - 1:
            finished.append(carried)
    returned_rows = broadcast(jnp.stack(finished), "section", sections - 1)
    final_hidden = lax.dynamic_index_in_dim(returned_rows, section_here, 0, keepdims=False)
    columns = row_grads.shape[1]
    picker = ((target == group_here)[:, None] & (position[:, None] == positions[None, :])).astype(
        jnp.bfloat16
    )
    outgoing = jnp.dot(picker, row_grads, preferred_element_type=jnp.float32).astype(jnp.bfloat16)
    outgoing = outgoing.reshape(dp_count, section_rows // dp_count, columns)
    returned = lax.all_to_all(
        lax.all_to_all(outgoing, "dp", split_axis=0, concat_axis=0, tiled=True),
        "mp",
        split_axis=1,
        concat_axis=2,
        tiled=True,
    )
    merged_grads = jnp.sum(returned.astype(jnp.float32), axis=0).astype(jnp.bfloat16)
    return (final_hidden, merged_grads)


def solution(mesh):
    in_specs = (
        P(("section", "dp", "mp"), None),
        P(("section", "dp", "mp"), None),
        P(),
        P(),
        P(),
        P(),
        P("dp", "mp"),
        P(("section", "dp", "mp"), None),
        P(("section", "dp"), "mp"),
        P(("section", "dp"), None),
        P("section", None),
        P("section", "dp", "mp"),
        P("section", "dp", "mp"),
        P(("section", "dp"), "mp"),
    )
    out_specs = (P(("section", "dp"), "mp"), P(("section", "dp", "mp"), None))
    return jax.shard_map(shards, mesh=mesh, in_specs=in_specs, out_specs=out_specs, check_vma=False)
```

profile of v0, /device:TPU:0, one launch (start us, length us, event | category | flops | bytes accessed | tf_op | source)
XLA Modules:
  0.0 799.6 jit_solution(8067572202809848577)
XLA Ops:
  9.6 6.6 convolution_convert_fusion.1
  34.4 24.9 %all-reduce = s32[1024]{0:T(1024)S(1)} all-reduce(s32[1024]{0:T(1024)S(1)} %bitcast_dynamic-update-slice_fusion), channel_id=1, replica_groups=mesh['section'=2,'dp'=16,'mp'=4] {'dp','mp'}, use_global_device_ids=true, to_apply=%add | all-reduce | flops 1024 | bytes 8192 | tf_op jit(solution)/shard_map/squeeze | solution.py:120
  60.4 60.5 %all-gather.9.cloned.1.call-done = bf16[1024,5120]{1,0:T(8,128)(2,1)} async-done(((bf16[16,5120]{1,0:T(8,128)(2,1)}), bf16[1024,5120]{1,0:T(8,128)(2,1)}) %all-gather.9.cloned.1.call-update) | async-done | bytes 10485776 | tf_op jit(solution)/shard_map/all_gather | solution.py:117
  120.9 10.7 %convolution_convert_fusion = bf16[2048,2048]{1,0:T(8,128)(2,1)} fusion(bf16[320,2048]{1,0:T(8,128)(2,1)} %param.20, s32[1024]{0:T(1024)S(1)} %get-tuple-element.7, bf16[1024,5120]{1,0:T(8,128)(2,1)} %all-gather.9.cloned.1.call-done, s32[]{:T(128)S(6)} %select_n.69), kind=kOutput, calls=%fused_computation.18 | convolution fusion | flops 4033478656 | bytes 10489860 | tf_op jit(solution)/shard_map/dot_general | solution.py:137
  132.4 83.8 %reduce-scatter.5.cloned.1.call-done = bf16[128,2048]{1,0:T(8,128)(2,1)} async-done(((bf16[2048,2048]{1,0:T(8,128)(2,1)}), bf16[128,2048]{1,0:T(8,128)(2,1)}) %reduce-scatter.5.cloned.1.call-update) | async-done | bytes 524304 | tf_op jit(solution)/shard_map/reduce_scatter | solution.py:136
  218.3 11.4 %all-gather.11.cloned.1.call-done = bf16[256,2048]{1,0:T(8,128)(2,1)} async-done(((bf16[128,2048]{1,0:T(8,128)(2,1)}), bf16[256,2048]{1,0:T(8,128)(2,1)}) %all-gather.11.cloned.1.call-update) | async-done | bytes 1048592 | tf_op jit(solution)/shard_map/all_gather | solution.py:157
  235.4 28.8 %all-gather.13.cloned.1.call-done = bf16[128,8192]{1,0:T(8,128)(2,1)} async-done(((bf16[128,2048]{1,0:T(8,128)(2,1)}), bf16[128,8192]{1,0:T(8,128)(2,1)}) %all-gather.13.cloned.1.call-update) | async-done | bytes 2097168 | tf_op jit(solution)/shard_map/all_gather | solution.py:171
  266.3 132.4 %all-gather.15.cloned.1.call-done = bf16[1,8192,1280]{2,1,0:T(8,128)(2,1)} async-done(((bf16[1,512,1280]{2,1,0:T(8,128)(2,1)}), bf16[1,8192,1280]{2,1,0:T(8,128)(2,1)}) %all-gather.15.cloned.1.call-update) | async-done | bytes 20971536 | tf_op jit(solution)/shard_map/all_gather | solution.py:146
  398.7 10.6 %fusion.35 = bf16[128,1280]{1,0:T(8,128)(2,1)S(1)} fusion(bf16[1,8192,1280]{2,1,0:T(8,128)(2,1)} %all-gather.15.cloned.1.call-done, bf16[128,8192]{1,0:T(8,128)(2,1)} %all-gather.13.cloned.1.call-done, f32[8192]{0:T(1024)S(1)} %bitcast.203, f32[128]{0:T(128)S(1)} %add_rsqrt_fusion.2), kind=kOutput, calls=%fused_computation.41 | convolution fusion | flops 2688712704 | bytes 23429632 | tf_op jit(solution)/shard_map/dot_general | solution.py:173
  410.1 101.6 %all-gather.17.cloned.1.call-done = bf16[1,8192,1024]{2,1,0:T(8,128)(2,1)} async-done(((bf16[1,512,1024]{2,1,0:T(8,128)(2,1)}), bf16[1,8192,1024]{2,1,0:T(8,128)(2,1)}) %all-gather.17.cloned.1.call-update) | async-done | bytes 16777232 | tf_op jit(solution)/shard_map/all_gather | solution.py:147
  511.7 12.8 %fusion.13 = bf16[128,8192]{1,0:T(8,128)(2,1)} fusion(bf16[128,1024]{0,1:T(8,128)(2,1)S(1)} %bitcast.197, bf16[1,8192,1024]{2,1,0:T(8,128)(2,1)} %all-gather.17.cloned.1.call-done), kind=kOutput, calls=%fused_computation.13 | convolution fusion | flops 2148532224 | bytes 19136512 | tf_op jit(solution)/shard_map/dot_general | solution.py:175
  524.6 29.7 %reduce-scatter.7.cloned.1.call-done = bf16[128,2048]{1,0:T(8,128)(2,1)} async-done(((bf16[128,8192]{1,0:T(8,128)(2,1)}), bf16[128,2048]{1,0:T(8,128)(2,1)}) %reduce-scatter.7.cloned.1.call-update) | async-done | bytes 524304 | tf_op jit(solution)/shard_map/reduce_scatter | solution.py:178
  563.2 27.3 %all-gather.19.cloned.1.call-done = bf16[128,8192]{1,0:T(8,128)(2,1)} async-done(((bf16[128,2048]{1,0:T(8,128)(2,1)}), bf16[128,8192]{1,0:T(8,128)(2,1)}) %all-gather.19.cloned.1.call-update) | async-done | bytes 2097168 | tf_op jit(solution)/shard_map/all_gather | solution.py:171
  592.6 10.6 %fusion.38 = bf16[128,1280]{1,0:T(8,128)(2,1)S(1)} fusion(bf16[1,8192,1280]{2,1,0:T(8,128)(2,1)} %all-gather.15.cloned.1.call-done, bf16[128,8192]{1,0:T(8,128)(2,1)} %all-gather.19.cloned.1.call-done, f32[128]{0:T(128)S(1)} %add_rsqrt_fusion.1, f32[8192]{0:T(1024)S(1)} %bitcast.204), kind=kOutput, calls=%fused_computation.42 | convolution fusion | flops 2688712704 | bytes 23429632 | tf_op jit(solution)/shard_map/dot_general | solution.py:173
  604.0 12.8 %fusion.16 = bf16[128,8192]{1,0:T(8,128)(2,1)} fusion(bf16[128,1024]{0,1:T(8,128)(2,1)S(1)} %bitcast.199, bf16[1,8192,1024]{2,1,0:T(8,128)(2,1)} %all-gather.17.cloned.1.call-done), kind=kOutput, calls=%fused_computation.14 | convolution fusion | flops 2148532224 | bytes 19136512 | tf_op jit(solution)/shard_map/dot_general | solution.py:175
  616.9 29.9 %reduce-scatter.9.cloned.1.call-done = bf16[128,2048]{1,0:T(8,128)(2,1)} async-done(((bf16[128,8192]{1,0:T(8,128)(2,1)}), bf16[128,2048]{1,0:T(8,128)(2,1)}) %reduce-scatter.9.cloned.1.call-update) | async-done | bytes 524304 | tf_op jit(solution)/shard_map/reduce_scatter | solution.py:178
  655.2 6.9 all-to-all-start
  665.3 17.6 %all-gather.21.cloned.1.call-done = bf16[128,8192]{1,0:T(8,128)(2,1)} async-done(((bf16[128,2048]{1,0:T(8,128)(2,1)}), bf16[128,8192]{1,0:T(8,128)(2,1)}) %all-gather.21.cloned.1.call-update) | async-done | bytes 2097168 | tf_op jit(solution)/shard_map/all_gather | solution.py:171
  685.0 10.6 %fusion.41 = bf16[128,1280]{1,0:T(8,128)(2,1)S(1)} fusion(bf16[1,8192,1280]{2,1,0:T(8,128)(2,1)} %all-gather.15.cloned.1.call-done, bf16[128,8192]{1,0:T(8,128)(2,1)} %all-gather.21.cloned.1.call-done, f32[128]{0:T(128)S(1)} %add_rsqrt_fusion, f32[8192]{0:T(1024)S(1)} %bitcast.205), kind=kOutput, calls=%fused_computation.43 | convolution fusion | flops 2688712704 | bytes 23429632 | tf_op jit(solution)/shard_map/dot_general | solution.py:173
  696.5 12.8 %fusion.19 = bf16[128,8192]{1,0:T(8,128)(2,1)} fusion(bf16[128,1024]{0,1:T(8,128)(2,1)S(1)} %bitcast.198, bf16[1,8192,1024]{2,1,0:T(8,128)(2,1)} %all-gather.17.cloned.1.call-done), kind=kOutput, calls=%fused_computation.15 | convolution fusion | flops 2148532224 | bytes 19136512 | tf_op jit(solution)/shard_map/dot_general | solution.py:175
  709.3 16.7 %all-to-all-done = bf16[16,64,2048]{2,1,0:T(8,128)(2,1)} async-done(((bf16[16,64,2048]{2,1,0:T(8,128)(2,1)}), bf16[16,64,2048]{2,1,0:T(8,128)(2,1)}, u32[]{:S(2)}, u32[]{:S(2)}) %all-to-all-start) | async-done | bytes 4194336 | tf_op jit(solution)/shard_map/all_to_all | solution.py:193
  726.0 6.5 copy.122
  732.5 5.0 all-to-all-start.1
  742.8 43.2 %all-to-all-done.1 = bf16[16,64,2048]{2,0,1:T(8,128)(2,1)} async-done(((bf16[16,64,2048]{2,0,1:T(8,128)(2,1)}), bf16[16,64,2048]{2,0,1:T(8,128)(2,1)}, u32[]{:S(2)}, u32[]{:S(2)}) %all-to-all-start.1) | async-done | bytes 4194336 | tf_op jit(solution)/shard_map/all_to_all | solution.py:192
  (137 shorter events, 70.5 us)
Async XLA Ops:
  7.2 113.7 %all-gather.9.cloned.1.call-start = ((), (), s32[]{:S(2)}) async-start(), calls=%async_computation.6 | async-start | bytes 10649600 | tf_op jit(solution)/shard_map/all_gather | solution.py:117
  32.9 183.3 %reduce-scatter.5.cloned.1.call-start = ((), (), s32[]{:S(2)}) async-start(), calls=%async_computation.7 | async-start | bytes 8912896 | tf_op jit(solution)/shard_map/reduce_scatter | solution.py:136
  131.6 84.6 %copy-start.9 = (bf16[128,2048]{1,0:T(8,128)(2,1)S(1)}, bf16[128,2048]{1,0:T(8,128)(2,1)}, u32[]{:S(2)}) copy-start(bf16[128,2048]{1,0:T(8,128)(2,1)} %param.22) | copy-start | bytes 1572868
  131.7 101.1 %copy-start.11 = (s32[1,3]{1,0:T(1,128)S(1)}, s32[1,3]{1,0:T(1,128)}, u32[]{:S(2)}) copy-start(s32[1,3]{1,0:T(1,128)} %param.23) | copy-start | bytes 40
  131.7 267.0 %copy-start.12 = (f32[1,8192]{1,0:T(1,128)S(1)}, f32[1,8192]{1,0:T(1,128)}, u32[]{:S(2)}) copy-start(f32[1,8192]{1,0:T(1,128)} %param.24) | copy-start | bytes 98308
  131.7 98.0 %all-gather.11.cloned.1.call-start = ((), (), s32[]{:S(2)}) async-start(), calls=%async_computation.8 | async-start | bytes 1572864 | tf_op jit(solution)/shard_map/all_gather | solution.py:157
  218.2 46.0 %all-gather.13.cloned.1.call-start = ((), (), s32[]{:S(2)}) async-start(), calls=%async_computation.9 | async-start | bytes 2621440 | tf_op jit(solution)/shard_map/all_gather | solution.py:171
  231.6 167.1 %all-gather.15.cloned.1.call-start = ((), (), s32[]{:S(2)}) async-start(), calls=%async_computation.10 | async-start | bytes 22282240 | tf_op jit(solution)/shard_map/all_gather | solution.py:146
  232.2 279.5 %all-gather.17.cloned.1.call-start = ((), (), s32[]{:S(2)}) async-start(), calls=%async_computation.11 | async-start | bytes 17825792 | tf_op jit(solution)/shard_map/all_gather | solution.py:147
  232.7 321.6 %reduce-scatter.7.cloned.1.call-start = ((), (), s32[]{:S(2)}) async-start(), calls=%async_computation.12 | async-start | bytes 2621440 | tf_op jit(solution)/shard_map/reduce_scatter | solution.py:178
  511.7 42.6 %copy-start.4 = (bf16[256,2048]{1,0:T(8,128)(2,1)S(1)}, bf16[256,2048]{1,0:T(8,128)(2,1)}, u32[]{:S(2)}) copy-start(bf16[256,2048]{1,0:T(8,128)(2,1)} %all-gather.11.cloned.1.call-done) | copy-start | bytes 3145732
  524.5 66.0 %all-gather.19.cloned.1.call-start = ((), (), s32[]{:S(2)}) async-start(), calls=%async_computation.13 | async-start | bytes 2621440 | tf_op jit(solution)/shard_map/all_gather | solution.py:171
  555.5 3.3 collective-permute-start
  559.7 87.1 %reduce-scatter.9.cloned.1.call-start = ((), (), s32[]{:S(2)}) async-start(), calls=%async_computation.14 | async-start | bytes 2621440 | tf_op jit(solution)/shard_map/reduce_scatter | solution.py:178
  559.8 3.1 collective-permute-start.1
  604.0 42.7 %copy-start.2 = (bf16[128,2048]{1,0:T(8,128)(2,1)S(1)}, bf16[128,2048]{1,0:T(8,128)(2,1)}, u32[]{:S(2)}) copy-start(bf16[128,2048]{1,0:T(8,128)(2,1)} %slice_select_fusion.1) | copy-start | bytes 1572868
  616.9 66.1 %all-gather.21.cloned.1.call-start = ((), (), s32[]{:S(2)}) async-start(), calls=%async_computation.15 | async-start | bytes 2621440 | tf_op jit(solution)/shard_map/all_gather | solution.py:171
  648.0 3.3 collective-permute-start.2
  655.2 70.8 %all-to-all-start = ((bf16[16,64,2048]{2,1,0:T(8,128)(2,1)}), bf16[16,64,2048]{2,1,0:T(8,128)(2,1)}, u32[]{:S(2)}, u32[]{:S(2)}) async-start(bf16[16,64,2048]{2,1,0:T(8,128)(2,1)} %bitcast.188), calls=%async_computation.4 | async-start | bytes 8388608 | tf_op jit(solution)/shard_map/all_to_all | solution.py:193
  662.1 77.1 %reduce-scatter.11.cloned.1.call-start = ((), (), s32[]{:S(2)}) async-start(), calls=%async_computation.16 | async-start | bytes 2621440 | tf_op jit(solution)/shard_map/reduce_scatter | solution.py:178
  662.1 2.8 collective-permute-start.3
  732.5 53.5 %all-to-all-start.1 = ((bf16[16,64,2048]{2,0,1:T(8,128)(2,1)}), bf16[16,64,2048]{2,0,1:T(8,128)(2,1)}, u32[]{:S(2)}, u32[]{:S(2)}) async-start(bf16[16,64,2048]{2,0,1:T(8,128)(2,1)} %copy.122), calls=%async_computation.5 | async-start | bytes 8388608 | tf_op jit(solution)/shard_map/all_to_all | solution.py:192
  737.5 53.2 %all-reduce.3.cloned.1.call-start = ((), (), s32[]{:S(2)}) async-start(), calls=%async_computation.17 | async-start | bytes 2097152 | tf_op jit(solution)/shard_map/psum | solution.py:25
  740.4 52.1 %copy-start.1 = (bf16[1280,1280]{1,0:T(8,128)(2,1)S(1)}, bf16[1280,1280]{1,0:T(8,128)(2,1)}, u32[]{:S(2)}) copy-start(bf16[1280,1280]{1,0:T(8,128)(2,1)} %param.18) | copy-start | bytes 9830404
  (11 other events, 127.5 us)
Sparse Core Ops, SparseCore 0:
  33.0 87.8 all-gather.8
  131.8 84.4 reduce-scatter.4
  218.5 11.1 all-gather.10
  231.8 32.4 all-gather.12
  266.2 132.4 all-gather.14
  400.7 110.9 all-gather.16
  524.7 29.5 reduce-scatter.6
  559.8 30.6 all-gather.18
  617.0 29.7 reduce-scatter.8
  652.2 30.6 all-gather.20
  709.4 29.7 reduce-scatter.10
  742.9 26.6 all-reduce.2
where the time goes:
time: 808 us; the launch traced here: 800 us
  waiting for transfers between devices  590 us (73%)
  matrix products  97.5 us (12%)
  blocking collectives  27.2 us (3%)
  other arithmetic  27.1 us (3%)
  local copies, waits for them, and re-layouts  21.7 us (3%)
  starting transfers between devices  20.7 us (3%)
  between operations  15.5 us (2%)
    all_gather x1, waiting for transfers between devices, shards(): lax.all_gather(w_qkv, 'dp', axis=1, tiled=True)  132 us
    all_gather x1, waiting for transfers between devices, shards(): lax.all_gather(wo_t, 'dp', axis=1, tiled=True)  102 us
    reduce_scatter x1, waiting for transfers between devices, shards(): lax.psum_scatter(jnp.dot(picked, w_merge, preferred_element_type=jnp.floa...  83.8 us
    all_gather x3, waiting for transfers between devices, shards(): features = lax.all_gather(carried, 'mp', axis=1, tiled=True)  73.8 us
    reduce_scatter x3, waiting for transfers between devices, shards(): lax.psum_scatter(partial_value.astype(jnp.bfloat16), 'mp', scatter_dimens...  61.3 us
    all_gather x1, waiting for transfers between devices, shards(): lax.all_gather(merged, ('dp', 'mp'), axis=0, tiled=True)  60.5 us
    all_to_all x1, waiting for transfers between devices, shards(): lax.all_to_all(lax.all_to_all(outgoing, 'dp', split_axis=0, concat_axis=0...  43.2 us
    dot_general x3, matrix products, shards(): lax.dot_general(attended, out_weight, (((1,), (1,)), ((), ())), preferred...  38.4 us
  transfers between devices with their start and end apart: 18, of which 17 were waited for; matrix products, arithmetic and copies ran while one was open for 8% of the time, Pallas kernels for 0%

commit v1 on v0

--- a/solution.py
+++ b/solution.py
@@ -168,7 +168,26 @@
             incoming_lengths = lengths_all[section_step]
             carried = jnp.where(is_first, incoming, carried)
             carried_lengths = jnp.where(is_first, incoming_lengths, carried_lengths)
-        features = lax.all_gather(carried, "mp", axis=1, tiled=True)
+        odd = lax.axis_size("mp")
+        item_now, then, field_out = (odd, lax.axis_index("mp"), carried.shape[1])
+        by_place = [(h, (h + 1) % item_now) for h in range(item_now)]
+        leaves = [(h, (h - 1) % item_now) for h in range(item_now)]
+        features = jnp.zeros(
+            (*carried.shape[:1], item_now * field_out, *carried.shape[2:]), carried.dtype
+        )
+        features = lax.dynamic_update_slice_in_dim(features, carried, then * field_out, axis=1)
+        after = inter = carried
+        outcome_arr = item_now // 2
+        for dd in range(1, outcome_arr + 1):
+            after = lax.ppermute(after, axis_name="mp", perm=by_place)
+            features = lax.dynamic_update_slice_in_dim(
+                features, after, (then - dd) % item_now * field_out, axis=1
+            )
+            if dd < item_now - outcome_arr:
+                inter = lax.ppermute(inter, "mp", leaves)
+                features = lax.dynamic_update_slice_in_dim(
+                    features, inter, (then + dd) % item_now * field_out, axis=1
+                )
         normed = rms_norm(features, norm_gain).astype(jnp.bfloat16)
         projected = jnp.dot(normed, qkv_weight, preferred_element_type=jnp.float32)
         attended = attend(projected.astype(jnp.bfloat16), carried_lengths)

time: 808 us -> 771 us (0.954)
  waiting for transfers between devices: 590 us -> 548 us
  starting transfers between devices: 20.7 us -> 31.1 us
    all_gather x3 -> x0, waiting for transfers between devices: 73.8 us -> none  [shards(): features = lax.all_gather(carried, 'mp', axis=1, tiled=True)]
    ppermute x0 -> x9, waiting for transfers between devices: none -> 59.3 us  [the longest x6 45.5 us: shards(): after = lax.ppermute(after, axis_name='mp', perm=by_place)]
    all_gather x1, waiting for transfers between devices: 132 us -> 102 us  [shards(): lax.all_gather(w_qkv, 'dp', axis=1, tiled=True)]
    ppermute x0 -> x9, starting transfers between devices: none -> 10.9 us  [the longest x3 7.65 us: shards(): inter = lax.ppermute(inter, 'mp', leaves)]
  transfers between devices with their start and end apart: 18 -> 24, of which waited for: 17 -> 22; matrix products, arithmetic and copies ran while one was open for 8% -> 8% of each run, Pallas kernels for 0% -> 0%
where the time goes in v1:
time: 771 us; the launch traced here: 762 us
  waiting for transfers between devices  548 us (71%)
  matrix products  95.4 us (12%)
  starting transfers between devices  31.1 us (4%)
  blocking collectives  26.7 us (3%)
  local copies, waits for them, and re-layouts  25.1 us (3%)
  other arithmetic  20.6 us (3%)
  between operations  15.3 us (2%)
    all_gather x1, waiting for transfers between devices, shards(): lax.all_gather(w_qkv, 'dp', axis=1, tiled=True)  102 us
    all_gather x1, waiting for transfers between devices, shards(): lax.all_gather(wo_t, 'dp', axis=1, tiled=True)  102 us
    reduce_scatter x1, waiting for transfers between devices, shards(): lax.psum_scatter(jnp.dot(picked, w_merge, preferred_element_type=jnp.floa...  84 us
    all_gather x1, waiting for transfers between devices, shards(): lax.all_gather(merged, ('dp', 'mp'), axis=0, tiled=True)  60.5 us
    reduce_scatter x3, waiting for transfers between devices, shards(): lax.psum_scatter(partial_value.astype(jnp.bfloat16), 'mp', scatter_dimens...  58.5 us
    all_to_all x1, waiting for transfers between devices, shards(): lax.all_to_all(lax.all_to_all(outgoing, 'dp', split_axis=0, concat_axis=0...  46.1 us
    ppermute x6, waiting for transfers between devices, shards(): after = lax.ppermute(after, axis_name='mp', perm=by_place)  45.5 us
    dot_general x3, matrix products, shards(): lax.dot_general(attended, out_weight, (((1,), (1,)), ((), ())), preferred...  38.3 us
  transfers between devices with their start and end apart: 24, of which 22 were waited for; matrix products, arithmetic and copies ran while one was open for 8% of the time, Pallas kernels for 0%

profile of v1, /device:TPU:0, one launch (start us, length us, event | category | flops | bytes accessed | tf_op | source)
XLA Modules:
  0.0 761.8 jit_solution(9126136771049095027)
XLA Ops:
  9.6 6.6 convolution_convert_fusion.1
  34.4 24.9 %all-reduce = s32[1024]{0:T(1024)S(1)} all-reduce(s32[1024]{0:T(1024)S(1)} %bitcast_dynamic-update-slice_fusion), channel_id=1, replica_groups=mesh['section'=2,'dp'=16,'mp'=4] {'dp','mp'}, use_global_device_ids=true, to_apply=%add | all-reduce | flops 1024 | bytes 8192 | tf_op jit(solution)/shard_map/squeeze | solution.py:120
  60.5 60.5 %all-gather.6.cloned.1.call-done = bf16[1024,5120]{1,0:T(8,128)(2,1)} async-done(((bf16[16,5120]{1,0:T(8,128)(2,1)}), bf16[1024,5120]{1,0:T(8,128)(2,1)}) %all-gather.6.cloned.1.call-update) | async-done | bytes 10485776 | tf_op jit(solution)/shard_map/all_gather | solution.py:117
  120.9 10.7 %convolution_convert_fusion = bf16[2048,2048]{1,0:T(8,128)(2,1)} fusion(bf16[320,2048]{1,0:T(8,128)(2,1)} %param.20, s32[1024]{0:T(1024)S(1)} %get-tuple-element.11, bf16[1024,5120]{1,0:T(8,128)(2,1)} %all-gather.6.cloned.1.call-done, s32[]{:T(128)S(6)} %select_n.116), kind=kOutput, calls=%fused_computation.18 | convolution fusion | flops 4033478656 | bytes 10489860 | tf_op jit(solution)/shard_map/dot_general | solution.py:137
  132.4 84.0 %reduce-scatter.5.cloned.1.call-done = bf16[128,2048]{1,0:T(8,128)(2,1)} async-done(((bf16[2048,2048]{1,0:T(8,128)(2,1)}), bf16[128,2048]{1,0:T(8,128)(2,1)}) %reduce-scatter.5.cloned.1.call-update) | async-done | bytes 524304 | tf_op jit(solution)/shard_map/reduce_scatter | solution.py:136
  219.6 10.2 %all-gather.8.cloned.1.call-done = bf16[256,2048]{1,0:T(8,128)(2,1)} async-done(((bf16[128,2048]{1,0:T(8,128)(2,1)}), bf16[256,2048]{1,0:T(8,128)(2,1)}) %all-gather.8.cloned.1.call-update) | async-done | bytes 1048592 | tf_op jit(solution)/shard_map/all_gather | solution.py:157
  236.5 10.2 %collective-permute-done = bf16[128,2048]{1,0:T(8,128)(2,1)S(1)} collective-permute-done((bf16[128,2048]{1,0:T(8,128)(2,1)S(1)}, bf16[128,2048]{1,0:T(8,128)(2,1)S(1)}, u32[]{:S(2)}, u32[]{:S(2)}) %collective-permute-start) | collective-permute-done | bytes 524320 | tf_op jit(solution)/shard_map/ppermute | solution.py:182
  250.1 11.8 %collective-permute-done.2 = bf16[128,2048]{1,0:T(8,128)(2,1)} collective-permute-done((bf16[128,2048]{1,0:T(8,128)(2,1)S(1)}, bf16[128,2048]{1,0:T(8,128)(2,1)}, u32[]{:S(2)}, u32[]{:S(2)}) %collective-permute-start.2) | collective-permute-done | bytes 524320 | tf_op jit(solution)/shard_map/ppermute | solution.py:182
  263.5 102.3 %all-gather.10.cloned.1.call-done = bf16[1,8192,1280]{2,1,0:T(8,128)(2,1)} async-done(((bf16[1,512,1280]{2,1,0:T(8,128)(2,1)}), bf16[1,8192,1280]{2,1,0:T(8,128)(2,1)}) %all-gather.10.cloned.1.call-update) | async-done | bytes 20971536 | tf_op jit(solution)/shard_map/all_gather | solution.py:146
  365.8 9.9 %fusion.35 = bf16[128,1280]{1,0:T(8,128)(2,1)S(1)} fusion(bf16[1,8192,1280]{2,1,0:T(8,128)(2,1)} %all-gather.10.cloned.1.call-done, bf16[128,8192]{1,0:T(8,128)(2,1)S(1)} %constant_dynamic-update-slice_fusion.8, f32[8192]{0:T(1024)S(1)} %bitcast.205, f32[128]{0:T(128)S(1)} %add_rsqrt_fusion.2), kind=kOutput, calls=%fused_computation.41 | convolution fusion | flops 2688712704 | bytes 23429632 | tf_op jit(solution)/shard_map/dot_general | solution.py:192
  376.6 102.2 %all-gather.12.cloned.1.call-done = bf16[1,8192,1024]{2,1,0:T(8,128)(2,1)} async-done(((bf16[1,512,1024]{2,1,0:T(8,128)(2,1)}), bf16[1,8192,1024]{2,1,0:T(8,128)(2,1)}) %all-gather.12.cloned.1.call-update) | async-done | bytes 16777232 | tf_op jit(solution)/shard_map/all_gather | solution.py:147
  478.8 12.7 %fusion.13 = bf16[128,8192]{1,0:T(8,128)(2,1)} fusion(bf16[128,1024]{0,1:T(8,128)(2,1)S(1)} %bitcast.197, bf16[1,8192,1024]{2,1,0:T(8,128)(2,1)} %all-gather.12.cloned.1.call-done), kind=kOutput, calls=%fused_computation.13 | convolution fusion | flops 2148532224 | bytes 19136512 | tf_op jit(solution)/shard_map/dot_general | solution.py:194
  491.6 29.7 %reduce-scatter.7.cloned.1.call-done = bf16[128,2048]{1,0:T(8,128)(2,1)} async-done(((bf16[128,8192]{1,0:T(8,128)(2,1)}), bf16[128,2048]{1,0:T(8,128)(2,1)}) %reduce-scatter.7.cloned.1.call-update) | async-done | bytes 524304 | tf_op jit(solution)/shard_map/reduce_scatter | solution.py:197
  548.2 9.2 %collective-permute-done.6 = bf16[128,2048]{1,0:T(8,128)(2,1)S(1)} collective-permute-done((bf16[128,2048]{1,0:T(8,128)(2,1)S(1)}, bf16[128,2048]{1,0:T(8,128)(2,1)S(1)}, u32[]{:S(2)}, u32[]{:S(2)}) %collective-permute-start.6) | collective-permute-done | bytes 524320 | tf_op jit(solution)/shard_map/ppermute | solution.py:182
  558.0 9.9 %fusion.38 = bf16[128,1280]{1,0:T(8,128)(2,1)S(1)} fusion(bf16[1,8192,1280]{2,1,0:T(8,128)(2,1)} %all-gather.10.cloned.1.call-done, bf16[128,8192]{1,0:T(8,128)(2,1)S(1)} %constant_dynamic-update-slice_fusion.4, f32[128]{0:T(128)S(1)} %add_rsqrt_fusion.1, f32[8192]{0:T(1024)S(1)} %bitcast.206), kind=kOutput, calls=%fused_computation.42 | convolution fusion | flops 2688712704 | bytes 23429632 | tf_op jit(solution)/shard_map/dot_general | solution.py:192
  568.8 12.7 %fusion.16 = bf16[128,8192]{1,0:T(8,128)(2,1)} fusion(bf16[128,1024]{0,1:T(8,128)(2,1)S(1)} %bitcast.199, bf16[1,8192,1024]{2,1,0:T(8,128)(2,1)} %all-gather.12.cloned.1.call-done), kind=kOutput, calls=%fused_computation.14 | convolution fusion | flops 2148532224 | bytes 19136512 | tf_op jit(solution)/shard_map/dot_general | solution.py:194
  581.6 28.7 %reduce-scatter.9.cloned.1.call-done = bf16[128,2048]{1,0:T(8,128)(2,1)} async-done(((bf16[128,8192]{1,0:T(8,128)(2,1)}), bf16[128,2048]{1,0:T(8,128)(2,1)}) %reduce-scatter.9.cloned.1.call-update) | async-done | bytes 524304 | tf_op jit(solution)/shard_map/reduce_scatter | solution.py:197
  618.0 6.9 all-to-all-start
  631.9 7.4 collective-permute-done.10
  645.9 9.9 %fusion.41 = bf16[128,1280]{1,0:T(8,128)(2,1)S(1)} fusion(bf16[1,8192,1280]{2,1,0:T(8,128)(2,1)} %all-gather.10.cloned.1.call-done, bf16[128,8192]{1,0:T(8,128)(2,1)S(1)} %constant_dynamic-update-slice_fusion, f32[128]{0:T(128)S(1)} %add_rsqrt_fusion, f32[8192]{0:T(1024)S(1)} %bitcast.207), kind=kOutput, calls=%fused_computation.43 | convolution fusion | flops 2688712704 | bytes 23429632 | tf_op jit(solution)/shard_map/dot_general | solution.py:192
  656.6 12.8 %fusion.19 = bf16[128,8192]{1,0:T(8,128)(2,1)} fusion(bf16[128,1024]{0,1:T(8,128)(2,1)S(1)} %bitcast.198, bf16[1,8192,1024]{2,1,0:T(8,128)(2,1)} %all-gather.12.cloned.1.call-done), kind=kOutput, calls=%fused_computation.15 | convolution fusion | flops 2148532224 | bytes 19136512 | tf_op jit(solution)/shard_map/dot_general | solution.py:194
  669.5 19.1 %all-to-all-done = bf16[16,64,2048]{2,1,0:T(8,128)(2,1)} async-done(((bf16[16,64,2048]{2,1,0:T(8,128)(2,1)}), bf16[16,64,2048]{2,1,0:T(8,128)(2,1)}, u32[]{:S(2)}, u32[]{:S(2)}) %all-to-all-start) | async-done | bytes 4194336 | tf_op jit(solution)/shard_map/all_to_all | solution.py:212
  688.6 6.5 copy.122
  702.4 46.1 %all-to-all-done.1 = bf16[16,64,2048]{2,0,1:T(8,128)(2,1)} async-done(((bf16[16,64,2048]{2,0,1:T(8,128)(2,1)}), bf16[16,64,2048]{2,0,1:T(8,128)(2,1)}, u32[]{:S(2)}, u32[]{:S(2)}) %all-to-all-start.1) | async-done | bytes 4194336 | tf_op jit(solution)/shard_map/all_to_all | solution.py:211
  (152 shorter events, 101.5 us)
Async XLA Ops:
  7.2 113.8 %all-gather.6.cloned.1.call-start = ((), (), s32[]{:S(2)}) async-start(), calls=%async_computation.6 | async-start | bytes 10649600 | tf_op jit(solution)/shard_map/all_gather | solution.py:117
  32.9 183.5 %reduce-scatter.5.cloned.1.call-start = ((), (), s32[]{:S(2)}) async-start(), calls=%async_computation.7 | async-start | bytes 8912896 | tf_op jit(solution)/shard_map/reduce_scatter | solution.py:136
  131.7 98.1 %all-gather.8.cloned.1.call-start = ((), (), s32[]{:S(2)}) async-start(), calls=%async_computation.8 | async-start | bytes 1572864 | tf_op jit(solution)/shard_map/all_gather | solution.py:157
  218.4 147.4 %all-gather.10.cloned.1.call-start = ((), (), s32[]{:S(2)}) async-start(), calls=%async_computation.9 | async-start | bytes 22282240 | tf_op jit(solution)/shard_map/all_gather | solution.py:146
  219.0 259.8 %all-gather.12.cloned.1.call-start = ((), (), s32[]{:S(2)}) async-start(), calls=%async_computation.10 | async-start | bytes 17825792 | tf_op jit(solution)/shard_map/all_gather | solution.py:147
  219.6 301.7 %reduce-scatter.7.cloned.1.call-start = ((), (), s32[]{:S(2)}) async-start(), calls=%async_computation.11 | async-start | bytes 2621440 | tf_op jit(solution)/shard_map/reduce_scatter | solution.py:197
  231.2 15.5 %collective-permute-start = (bf16[128,2048]{1,0:T(8,128)(2,1)S(1)}, bf16[128,2048]{1,0:T(8,128)(2,1)S(1)}, u32[]{:S(2)}, u32[]{:S(2)}) collective-permute-start(bf16[128,2048]{1,0:T(8,128)(2,1)S(1)} %get-tuple-element.5), channel_id=1, source_target_pairs={{0,1},{1,2},{2,3},{3,0},{4,5},{5,6},{6,7},{7,4},{8,9},{9,10},{10,1... | collective-permute-start | bytes 1572872 | tf_op jit(solution)/shard_map/ppermute | solution.py:182
  234.9 14.1 %collective-permute-start.1 = (bf16[128,2048]{1,0:T(8,128)(2,1)S(1)}, bf16[128,2048]{1,0:T(8,128)(2,1)}, u32[]{:S(2)}, u32[]{:S(2)}) collective-permute-start(bf16[128,2048]{1,0:T(8,128)(2,1)S(1)} %get-tuple-element.5), channel_id=1, source_target_pairs={{0,3},{1,0},{2,1},{3,2},{4,7},{5,4},{6,5},{7,6},{8,11},{9,8},{10,9... | collective-permute-start | bytes 1572872 | tf_op jit(solution)/shard_map/ppermute | solution.py:187
  246.7 15.2 %collective-permute-start.2 = (bf16[128,2048]{1,0:T(8,128)(2,1)S(1)}, bf16[128,2048]{1,0:T(8,128)(2,1)}, u32[]{:S(2)}, u32[]{:S(2)}) collective-permute-start(bf16[128,2048]{1,0:T(8,128)(2,1)S(1)} %collective-permute-done), channel_id=1, source_target_pairs={{0,1},{1,2},{2,3},{3,0},{4,5},{5,6},{6,7},{7,4},{8,9},{9,10},{10,1... | collective-permute-start | bytes 1572872 | tf_op jit(solution)/shard_map/ppermute | solution.py:182
  491.5 118.8 %reduce-scatter.9.cloned.1.call-start = ((), (), s32[]{:S(2)}) async-start(), calls=%async_computation.12 | async-start | bytes 2621440 | tf_op jit(solution)/shard_map/reduce_scatter | solution.py:197
  522.5 3.3 collective-permute-start.3
  527.2 15.5 %collective-permute-start.4 = (bf16[128,2048]{1,0:T(8,128)(2,1)S(1)}, bf16[128,2048]{1,0:T(8,128)(2,1)S(1)}, u32[]{:S(2)}, u32[]{:S(2)}) collective-permute-start(bf16[128,2048]{1,0:T(8,128)(2,1)S(1)} %get-tuple-element.3), channel_id=1, source_target_pairs={{0,1},{1,2},{2,3},{3,0},{4,5},{5,6},{6,7},{7,4},{8,9},{9,10},{10,1... | collective-permute-start | bytes 1572872 | tf_op jit(solution)/shard_map/ppermute | solution.py:182
  527.5 2.9 collective-permute-start.7
  530.4 3.0 collective-permute-start.12
  533.6 14.6 %collective-permute-start.5 = (bf16[128,2048]{1,0:T(8,128)(2,1)S(1)}, bf16[128,2048]{1,0:T(8,128)(2,1)S(1)}, u32[]{:S(2)}, u32[]{:S(2)}) collective-permute-start(bf16[128,2048]{1,0:T(8,128)(2,1)S(1)} %get-tuple-element.3), channel_id=1, source_target_pairs={{0,3},{1,0},{2,1},{3,2},{4,7},{5,4},{6,5},{7,6},{8,11},{9,8},{10,9... | collective-permute-start | bytes 1572872 | tf_op jit(solution)/shard_map/ppermute | solution.py:187
  542.7 14.7 %collective-permute-start.6 = (bf16[128,2048]{1,0:T(8,128)(2,1)S(1)}, bf16[128,2048]{1,0:T(8,128)(2,1)S(1)}, u32[]{:S(2)}, u32[]{:S(2)}) collective-permute-start(bf16[128,2048]{1,0:T(8,128)(2,1)S(1)} %collective-permute-done.4), channel_id=1, source_target_pairs={{0,1},{1,2},{2,3},{3,0},{4,5},{5,6},{6,7},{7,4},{8,9},{9,10},{10,1... | collective-permute-start | bytes 1572872 | tf_op jit(solution)/shard_map/ppermute | solution.py:182
  611.5 3.3 collective-permute-start.8
  614.8 15.5 %collective-permute-start.9 = (bf16[128,2048]{1,0:T(8,128)(2,1)S(1)}, bf16[128,2048]{1,0:T(8,128)(2,1)}, u32[]{:S(2)}, u32[]{:S(2)}) collective-permute-start(bf16[128,2048]{1,0:T(8,128)(2,1)S(1)} %collective-permute-done.8), channel_id=1, source_target_pairs={{0,1},{1,2},{2,3},{3,0},{4,5},{5,6},{6,7},{7,4},{8,9},{9,10},{10,1... | collective-permute-start | bytes 1572872 | tf_op jit(solution)/shard_map/ppermute | solution.py:182
  618.0 70.5 %all-to-all-start = ((bf16[16,64,2048]{2,1,0:T(8,128)(2,1)}), bf16[16,64,2048]{2,1,0:T(8,128)(2,1)}, u32[]{:S(2)}, u32[]{:S(2)}) async-start(bf16[16,64,2048]{2,1,0:T(8,128)(2,1)} %bitcast.188), calls=%async_computation.4 | async-start | bytes 8388608 | tf_op jit(solution)/shard_map/all_to_all | solution.py:212
  624.9 75.2 %reduce-scatter.11.cloned.1.call-start = ((), (), s32[]{:S(2)}) async-start(), calls=%async_computation.13 | async-start | bytes 2621440 | tf_op jit(solution)/shard_map/reduce_scatter | solution.py:197
  625.0 14.3 %collective-permute-start.10 = (bf16[128,2048]{1,0:T(8,128)(2,1)S(1)}, bf16[128,2048]{1,0:T(8,128)(2,1)S(1)}, u32[]{:S(2)}, u32[]{:S(2)}) collective-permute-start(bf16[128,2048]{1,0:T(8,128)(2,1)S(1)} %collective-permute-done.8), channel_id=1, source_target_pairs={{0,3},{1,0},{2,1},{3,2},{4,7},{5,4},{6,5},{7,6},{8,11},{9,8},{10,9... | collective-permute-start | bytes 1572872 | tf_op jit(solution)/shard_map/ppermute | solution.py:187
  630.3 15.0 %collective-permute-start.11 = (bf16[128,2048]{1,0:T(8,128)(2,1)}, bf16[128,2048]{1,0:T(8,128)(2,1)S(1)}, u32[]{:S(2)}, u32[]{:S(2)}) collective-permute-start(bf16[128,2048]{1,0:T(8,128)(2,1)} %collective-permute-done.9), channel_id=1, source_target_pairs={{0,1},{1,2},{2,3},{3,0},{4,5},{5,6},{6,7},{7,4},{8,9},{9,10},{10,1... | collective-permute-start | bytes 1572872 | tf_op jit(solution)/shard_map/ppermute | solution.py:182
  695.0 53.4 %all-to-all-start.1 = ((bf16[16,64,2048]{2,0,1:T(8,128)(2,1)}), bf16[16,64,2048]{2,0,1:T(8,128)(2,1)}, u32[]{:S(2)}, u32[]{:S(2)}) async-start(bf16[16,64,2048]{2,0,1:T(8,128)(2,1)} %copy.122), calls=%async_computation.5 | async-start | bytes 8388608 | tf_op jit(solution)/shard_map/all_to_all | solution.py:211
  700.0 53.1 %all-reduce.3.cloned.1.call-start = ((), (), s32[]{:S(2)}) async-start(), calls=%async_computation.14 | async-start | bytes 2097152 | tf_op jit(solution)/shard_map/psum | solution.py:25
  (14 other events, 411.1 us)
Sparse Core Ops, SparseCore 0:
  33.1 87.8 all-gather.5
  131.8 84.5 reduce-scatter.4
  218.6 11.1 all-gather.7
  231.8 133.9 all-gather.9
  367.8 110.9 all-gather.11
  491.7 29.5 reduce-scatter.6
  581.7 28.5 reduce-scatter.8
  669.6 28.5 reduce-scatter.10
  703.5 24.9 all-reduce.2
